TPU v7x, 32 devices: a whole 2x2x4 slice. The times are simulated.
32 devices in a mesh: dp: 4 (over z), tensor: 4 (over y, x), seq: 2 (over core).
Axes of the slice: x: 2, y: 2, z: 4, core: 2. Of those that a mesh axis runs over, the one named last changes fastest.
Arguments:
- hidden: bfloat16 [1024, 4096], P(('dp', 'seq'), 'tensor'), may hold values from -6 to 6
- w_in: bfloat16 [4096, 512], P('tensor'), may hold values from -0.09375 to 0.09375
- embed: bfloat16 [1024, 512], replicated, may hold values from -16 to 16
- gain: float32 [512], replicated, may hold values from 0.1 to 1.9
- w_head: bfloat16 [512, 1024], replicated, may hold values from -2 to 2
- tokens: int32 [1024, 8], P(('dp', 'seq')), may hold values from 0 to 1023
- frame_mask: int32 [1024], P(('dp', 'seq')), may hold values from 0 to 1, as said below
Outputs:
- loss: float32 [], replicated
- grad_head: float32 [524288], P(('dp', 'tensor', 'seq'))
- grad_hidden: bfloat16 [1024, 4096], P(('dp', 'seq'), 'tensor')
Inputs may be any that keep to these rules, and one draw needn't show every extreme that they name: `frame_mask`: frame 0 always counts.
All inputs are finite; a program needn't handle non-finite values.
Results may differ from a plain program's by a relative error of at most 0.015.
Values may be sent and summed in bfloat16 or wider, within the bound.
A program may use at most 64 MiB of HBM per device.

v0:
```python
import functools

import jax
import jax.numpy as jnp
from jax import lax
from jax.experimental import pallas as pl
from jax.experimental.pallas import tpu as pltpu
from jax.sharding import PartitionSpec as P

F32 = jnp.float32
BF16 = jnp.bfloat16
MESH = pl.DeviceIdType.MESH


def decode_terms(context, tok_rows, mask_rows, embed, gain, w_head, count_fn):
    frames = context.shape[0]
    width = context.shape[1]
    steps = tok_rows.shape[1]
    before = embed[tok_rows[:, :-1]].astype(jnp.float32)
    leading = jnp.zeros((frames, 1, width), jnp.float32)
    inputs = context.astype(jnp.float32)[:, None, :] + jnp.concatenate([leading, before], 1)
    inverse = lax.rsqrt(jnp.mean(inputs * inputs, -1, keepdims=True) + 1e-06)
    normed = inputs * inverse
    scaled = (normed * gain).astype(jnp.bfloat16)
    flat = scaled.reshape(frames * steps, width)
    logits = jnp.dot(flat, w_head, preferred_element_type=jnp.float32)
    top = jnp.max(logits, -1, keepdims=True)
    total = top[:, 0] + jnp.log(jnp.sum(jnp.exp(logits - top), -1))
    target = tok_rows.reshape(-1)
    onehot = (target[:, None] == jnp.arange(w_head.shape[1], dtype=jnp.int32)[None, :]).astype(
        jnp.float32
    )
    nll = total - jnp.sum(logits * onehot, -1)
    weights = (mask_rows.astype(jnp.float32)[:, None] * jnp.ones((1, steps), jnp.float32)).reshape(
        -1
    )
    count, loss_sum = count_fn(
        steps * jnp.sum(mask_rows.astype(jnp.float32)), jnp.sum(weights * nll)
    )
    probs = jnp.exp(logits - total[:, None])
    grad_logits = ((probs - onehot) * weights[:, None] / count).astype(jnp.bfloat16)
    head_term = lax.dot_general(
        flat, grad_logits, (((0,), (0,)), ((), ())), preferred_element_type=jnp.float32
    )
    grad_scaled = lax.dot_general(
        grad_logits, w_head, (((1,), (1,)), ((), ())), preferred_element_type=jnp.float32
    )
    scaled_grad = grad_scaled.reshape(inputs.shape) * gain
    grad_inputs = inverse * (
        scaled_grad - normed * jnp.mean(scaled_grad * normed, -1, keepdims=True)
    )
    grad_context = jnp.sum(grad_inputs, 1).astype(jnp.bfloat16)
    return (loss_sum / count, head_term, grad_context)


def add_totals(count_local, loss_local):
    return lax.psum((count_local, loss_local), ("dp", "tensor", "seq"))


def per_device_plain(hidden, w_in, embed, gain, w_head, tokens, frame_mask):
    groups = lax.axis_size("tensor")
    rows = hidden.shape[0] // groups
    context = lax.psum_scatter(
        jnp.dot(hidden, w_in, preferred_element_type=jnp.float32),
        "tensor",
        scatter_dimension=0,
        tiled=True,
    ).astype(jnp.bfloat16)
    offset = lax.axis_index("tensor") * rows
    tok_rows = lax.dynamic_slice_in_dim(tokens, offset, rows, 0)
    mask_rows = lax.dynamic_slice_in_dim(frame_mask, offset, rows, 0)
    loss, head_term, grad_context = decode_terms(
        context, tok_rows, mask_rows, embed, gain, w_head, add_totals
    )
    flat_term = head_term.reshape(-1)
    partial_grad = lax.psum_scatter(
        flat_term.astype(jnp.bfloat16), "dp", scatter_dimension=0, tiled=True
    ).astype(jnp.float32)
    grad_head = lax.psum_scatter(partial_grad, ("tensor", "seq"), scatter_dimension=0, tiled=True)
    product = lax.dot_general(
        lax.all_gather(grad_context, "tensor", axis=0, tiled=True),
        w_in,
        (((1,), (1,)), ((), ())),
        preferred_element_type=jnp.float32,
    )
    grad_hidden = product.astype(jnp.bfloat16)
    return (loss, grad_head, grad_hidden)


def kernel(
    sizes, hidden_h, w_in_h, embed_h, gain_h, w_head_h, tokens_h, mask_h,
    loss_o, head_o, gh_o,
    hidden, w_in, embed, gain, w_head, tokens, mask,
    ctx_own, ctx_send, ctx_recv, cnt, cnt_recv, gath, scaled, gl, hs, r1, s1, r2, s2, r3,
    gc, ls1, ls1_r, ls2, ls2_r, ls3, ls3_r,
    in_sem, ctx_ss, ctx_rs, cnt_ss, cnt_rs, gc_ss, gc_rs,
    h1_ss, h1_rs, h2_ss, h2_rs, h3_ss, h3_rs, l_ss, l_rs,
):
    DP, T, S = sizes
    a, t, s = lax.axis_index("dp"), lax.axis_index("tensor"), lax.axis_index("seq")
    steps, nframes = tokens.shape
    frames = nframes // T
    width, vocab = w_head.shape
    rows = frames * steps
    piece = width // (DP * T * S)

    barrier = pltpu.get_barrier_semaphore()
    peers_t = [{"tensor": lax.rem(t + d, T)} for d in range(1, T)]
    peers_g = [
        {"dp": lax.rem(a + d, DP), "seq": lax.rem(s + e, S)}
        for d in range(DP)
        for e in range(S)
        if d or e
    ]
    for peer in peers_t + peers_g:
        pl.semaphore_signal(barrier, inc=1, device_id=peer, device_id_type=MESH)

    loads = [
        pltpu.make_async_copy(src, dst, in_sem.at[i])
        for i, (src, dst) in enumerate(
            [
                (hidden_h, hidden),
                (w_in_h, w_in),
                (mask_h, mask),
                (tokens_h, tokens),
                (embed_h, embed),
                (gain_h, gain),
                (w_head_h, w_head),
            ]
        )
    ]
    for load in loads:
        load.start()

    sends, seen = [], set()

    def got(copy):
        copy.wait_recv()
        seen.add(id(copy))

    def send(src, dst, ss, rs, peer):
        copy = pltpu.make_async_remote_copy(
            src_ref=src, dst_ref=dst, send_sem=ss, recv_sem=rs, device_id=peer, device_id_type=MESH
        )
        copy.start()
        sends.append(copy)
        return copy

    loads[0].wait()
    loads[1].wait()
    part = jnp.dot(hidden[...], w_in[...], preferred_element_type=F32).reshape(T, frames, width)
    ctx_send[...] = part.astype(BF16)
    ctx_own[...] = part
    loads[2].wait()
    mask_row = mask[...].astype(F32)
    cnt[...] = jnp.zeros(cnt.shape, F32) + jnp.sum(mask_row)
    pl.semaphore_wait(barrier, len(peers_t) + len(peers_g))
    ctx_copies = [
        send(ctx_send.at[lax.rem(t + d, T)], ctx_recv.at[d - 1], ctx_ss.at[d - 1], ctx_rs.at[d - 1],
             peers_t[d - 1])
        for d in range(1, T)
    ]
    cnt_copies = [
        send(cnt, cnt_recv.at[i], cnt_ss.at[i], cnt_rs.at[i], peer) for i, peer in enumerate(peers_g)
    ]

    loads[3].wait()
    spot = lax.broadcasted_iota(jnp.int32, (frames, nframes), 0) + t * frames
    here = lax.broadcasted_iota(jnp.int32, (frames, nframes), 1)
    mine = spot == here
    tok = tokens[...].astype(F32)
    lanes = lax.broadcasted_iota(jnp.int32, (frames, vocab), 1).astype(F32)
    hot = [
        jnp.sum(jnp.where(mine, tok[k : k + 1, :], 0.0), 1, keepdims=True) == lanes
        for k in range(steps)
    ]
    loads[4].wait()
    prev = jnp.concatenate([jnp.where(h, 1.0, 0.0).astype(BF16) for h in hot[:-1]], 0)
    gath[...] = jnp.dot(prev, embed[...], preferred_element_type=F32)
    mcol = jnp.sum(jnp.where(mine, mask_row, 0.0), 1, keepdims=True)
    loads[5].wait()
    loads[6].wait()
    gvec = gain[...]

    ctx = ctx_own[t]
    for d in range(1, T):
        got(ctx_copies[d - 1])
        ctx = ctx + ctx_recv[d - 1].astype(F32)
    ctx = ctx.astype(BF16).astype(F32)
    inputs = jnp.concatenate([ctx] * steps, 0) + jnp.concatenate(
        [jnp.zeros((frames, width), F32), gath[...]], 0
    )
    inverse = lax.rsqrt(jnp.mean(inputs * inputs, -1, keepdims=True) + 1e-06)
    normed = inputs * inverse
    flat = (normed * gvec).astype(BF16)
    scaled[...] = flat
    logits = jnp.dot(flat, w_head[...], preferred_element_type=F32)
    top = jnp.max(logits, -1, keepdims=True)
    powers = jnp.exp(logits - top)
    norm = jnp.sum(powers, -1, keepdims=True)
    total = top + jnp.log(norm)
    onehot = jnp.concatenate([jnp.where(h, 1.0, 0.0) for h in hot], 0)
    weights = jnp.concatenate([mcol] * steps, 0)
    nll = total - jnp.sum(logits * onehot, -1, keepdims=True)
    grads = ((powers * (1.0 / norm) - onehot) * weights).astype(BF16)
    gl[...] = grads

    chunk = width // DP
    order = []
    for j in range(DP - 1):
        up = jnp.where(j < a, j, j + 1)
        down = jnp.where(DP - 1 - j > a, DP - 1 - j, DP - 2 - j)
        order.append(jnp.where(2 * a < DP, down, up))
    order.append(a)
    h1, h2 = [], []

    def tensor_stage(j):
        acc = hs[j, :, s].astype(F32)
        for e in range(1, S):
            got(h1[j * (S - 1) + e - 1])
            acc = acc + r1[j, e - 1].astype(F32)
        s1[j] = acc.astype(BF16)
        for d in range(1, T):
            h2.append(
                send(s1.at[j, lax.rem(t + d, T)], r2.at[j, d - 1], h2_ss.at[j, d - 1],
                     h2_rs.at[j, d - 1], peers_t[d - 1])
            )

    lag = 1
    for j in range(DP):
        c = order[j]
        cols = scaled[:, pl.ds(pl.multiple_of(c * chunk, chunk), chunk)]
        term = lax.dot_general(
            cols, gl[...], (((0,), (0,)), ((), ())), preferred_element_type=F32
        )
        hs[j] = term.astype(BF16).reshape(T, S, piece, vocab)
        for e in range(1, S):
            h1.append(
                send(hs.at[j, :, lax.rem(s + e, S)], r1.at[j, e - 1], h1_ss.at[j, e - 1],
                     h1_rs.at[j, e - 1], {"seq": lax.rem(s + e, S)})
            )
        if j >= lag:
            tensor_stage(j - lag)
    for j in range(max(DP - lag, 0), DP):
        tensor_stage(j)
    ls1[...] = jnp.zeros(ls1.shape, F32) + jnp.sum(weights * nll)
    n = 0
    lc1 = []
    for e in range(1, S):
        lc1.append(send(ls1, ls1_r.at[e - 1], l_ss.at[n], l_rs.at[n], {"seq": lax.rem(s + e, S)}))
        n += 1

    lsum = ls1[...]
    for e in range(1, S):
        got(lc1[e - 1])
        lsum = lsum + ls1_r[e - 1]
    ls2[...] = lsum
    lc2 = []
    for d in range(1, T):
        lc2.append(send(ls2, ls2_r.at[d - 1], l_ss.at[n], l_rs.at[n], peers_t[d - 1]))
        n += 1

    grad_scaled = lax.dot_general(
        gl[...], w_head[...], (((1,), (1,)), ((), ())), preferred_element_type=F32
    )
    g = grad_scaled * gvec
    gi = inverse * (g - normed * jnp.mean(g * normed, -1, keepdims=True))
    gsum = gi[0:frames]
    for k in range(1, steps):
        gsum = gsum + gi[k * frames : (k + 1) * frames]
    gc[t] = gsum.astype(BF16)
    gc_copies = [
        send(gc.at[t], gc.at[t], gc_ss.at[d - 1], gc_rs.at[d - 1], peers_t[d - 1])
        for d in range(1, T)
    ]

    h3 = []
    for j in range(DP):
        acc = s1[j, t].astype(F32)
        for d in range(1, T):
            got(h2[j * (T - 1) + d - 1])
            acc = acc + r2[j, d - 1].astype(F32)
        if j < DP - 1:
            s2[j] = acc.astype(BF16)
            slot = lax.rem(order[j] - a + DP, DP) - 1
            h3.append(
                send(s2.at[j], r3.at[slot], h3_ss.at[j], h3_rs.at[slot], {"dp": order[j]})
            )
    lsum = ls2[...]
    for d in range(1, T):
        got(lc2[d - 1])
        lsum = lsum + ls2_r[d - 1]
    ls3[...] = lsum
    lc3 = []
    for d in range(1, DP):
        lc3.append(
            send(ls3, ls3_r.at[d - 1], l_ss.at[n], l_rs.at[n], {"dp": lax.rem(a + d, DP)})
        )
        n += 1
    total_mask = cnt[...]
    for i in range(len(peers_g)):
        got(cnt_copies[i])
        total_mask = total_mask + cnt_recv[i]
    share = 1.0 / (total_mask[0:1, 0:1] * steps)
    for d in range(1, T):
        got(gc_copies[d - 1])
    product = lax.dot_general(
        gc[...].reshape(nframes, width), w_in[...], (((1,), (1,)), ((), ())),
        preferred_element_type=F32,
    )
    gh_o[...] = (product * share).astype(BF16)

    for j in range(DP - 1):
        arrival = pltpu.make_async_remote_copy(
            src_ref=s2.at[j], dst_ref=r3.at[j], send_sem=h3_ss.at[j], recv_sem=h3_rs.at[j],
            device_id={"dp": lax.rem(a + 1, DP)}, device_id_type=MESH,
        )
        arrival.wait_recv()
        acc = acc + r3[j].astype(F32)
    acc = acc * share
    groups = vocab // 128
    for b in range(groups):
        head_o[pl.ds(b, piece, stride=groups), :] = acc[:, b * 128 : (b + 1) * 128]
    for d in range(1, DP):
        got(lc3[d - 1])
        lsum = lsum + ls3_r[d - 1]
    loss_o[...] = lsum[0:1, 0:1] * share
    for copy in sends:
        copy.wait_send()


def write_out(loss_i, head_i, gh_i, loss_o, head_o, gh_o, sem):
    copies = [
        pltpu.make_async_copy(src, dst, sem.at[i])
        for i, (src, dst) in enumerate([(gh_i, gh_o), (head_i, head_o), (loss_i, loss_o)])
    ]
    for copy in copies:
        copy.start()
    for copy in copies:
        copy.wait()


def per_device_kernel(hidden, w_in, embed, gain, w_head, tokens, frame_mask):
    DP, T, S = lax.axis_size("dp"), lax.axis_size("tensor"), lax.axis_size("seq")
    nframes, feats = hidden.shape
    steps = tokens.shape[1]
    frames = nframes // T
    width, vocab = w_head.shape
    rows = frames * steps
    piece = width // (DP * T * S)
    G = DP * S - 1
    V = pltpu.VMEM
    dma = pltpu.SemaphoreType.DMA
    scratch = [
        V(hidden.shape, BF16), V(w_in.shape, BF16), V(embed.shape, BF16), V((1, width), F32),
        V(w_head.shape, BF16), V((steps, nframes), jnp.int32), V((1, nframes), jnp.int32),
        V((T, frames, width), F32),
        V((T, frames, width), BF16),
        V((T - 1, frames, width), BF16),
        V((8, 128), F32),
        V((G, 8, 128), F32),
        V((rows - frames, width), F32),
        V((rows, width), BF16),
        V((rows, vocab), BF16),
        V((DP, T, S, piece, vocab), BF16),
        V((DP, S - 1, T, piece, vocab), BF16),
        V((DP, T, piece, vocab), BF16),
        V((DP, T - 1, piece, vocab), BF16),
        V((DP - 1, piece, vocab), BF16),
        V((DP - 1, piece, vocab), BF16),
        V((T, frames, width), BF16),
        V((8, 128), F32), V((S - 1, 8, 128), F32),
        V((8, 128), F32), V((T - 1, 8, 128), F32),
        V((8, 128), F32), V((DP - 1, 8, 128), F32),
        dma((7,)),
        dma((T - 1,)), dma((T - 1,)), dma((G,)), dma((G,)), dma((T - 1,)), dma((T - 1,)),
        dma((DP, S - 1)), dma((DP, S - 1)), dma((DP, T - 1)), dma((DP, T - 1)),
        dma((DP - 1,)), dma((DP - 1,)), dma((S + T + DP - 3,)), dma((S + T + DP - 3,)),
    ]
    shapes = (
        jax.ShapeDtypeStruct((1, 1), F32),
        jax.ShapeDtypeStruct((piece * vocab // 128, 128), F32),
        jax.ShapeDtypeStruct((nframes, feats), BF16),
    )
    vmem = pl.BlockSpec(memory_space=pltpu.VMEM)
    results = pl.pallas_call(
        functools.partial(kernel, (DP, T, S)),
        out_shape=shapes,
        in_specs=[pl.BlockSpec(memory_space=pltpu.HBM)] * 7,
        out_specs=(vmem, vmem, vmem),
        scratch_shapes=scratch,
        compiler_params=pltpu.CompilerParams(
            collective_id=0, has_side_effects=True, vmem_limit_bytes=40 << 20
        ),
        name="decode",
    )(*[pltpu.with_memory_space_constraint(x, pltpu.HBM) for x in (hidden, w_in, embed, gain.reshape(1, -1), w_head, tokens.T, frame_mask.reshape(1, -1))])
    loss, head, grad_hidden = pl.pallas_call(
        write_out,
        out_shape=shapes,
        in_specs=[pl.BlockSpec(memory_space=pl.ANY)] * 3,
        out_specs=(pl.BlockSpec(memory_space=pltpu.HBM),) * 3,
        scratch_shapes=[dma((3,))],
        compiler_params=pltpu.CompilerParams(vmem_limit_bytes=4 << 20),
        name="write_out",
    )(*results)
    return loss.reshape(()), head.reshape(-1), grad_hidden


def solution(mesh):
    def per_device(hidden, w_in, embed, gain, w_head, tokens, frame_mask):
        DP, T, S = mesh.shape["dp"], mesh.shape["tensor"], mesh.shape["seq"]
        width, vocab = w_head.shape
        fits = (
            width % (16 * DP * T * S) == 0
            and width % (128 * DP) == 0
            and vocab % 128 == 0
            and hidden.shape[0] % (16 * T) == 0
            and min(DP, T, S) > 1
        )
        run = per_device_kernel if fits else per_device_plain
        return run(hidden, w_in, embed, gain, w_head, tokens, frame_mask)

    placed = (
        P(("dp", "seq"), "tensor"),
        P("tensor", None),
        P(),
        P(),
        P(),
        P(("dp", "seq"), None),
        P(("dp", "seq")),
    )
    return jax.shard_map(
        per_device,
        mesh=mesh,
        in_specs=placed,
        out_specs=(P(), P(("dp", "tensor", "seq")), P(("dp", "seq"), "tensor")),
        check_vma=False,
    )
```

profile of v0, /device:TPU:0, one launch (start us, length us, event | category | flops | bytes accessed | tf_op | source)
XLA Modules:
  0.0 25.9 jit_solution(1636471244529271298)
XLA Ops:
  0.6 23.9 %decode.1 = (f32[1,1]{1,0:T(1,128)}, f32[128,128]{1,0:T(8,128)S(1)}, bf16[128,1024]{1,0:T(8,128)(2,1)S(1)}) custom-call(bf16[128,1024]{1,0:T(8,128)(2,1)} %hidden_h.1, bf16[1024,512]{1,0:T(8,128)(2,1)} %w_in_h.1, bf16[1024,512]{1,0:T(8,128)(2,1)} %embed_h.1, f32[1,512]{1,0:T(1,128)} %bitcast.6, bf16[512,1024]{1,0:T(8,128)(2,1)} %w_head_h.1, ...), custom_call_target="tpu_custom_call" | custom-call | tf_op jit(solution)/shard_map/decode/pallas_call | solution.py:386
  24.5 1.4 %write_out.1 = (f32[1,1]{1,0:T(1,128)}, f32[128,128]{1,0:T(8,128)}, bf16[128,1024]{1,0:T(8,128)(2,1)}) custom-call(f32[1,1]{1,0:T(1,128)} %get-tuple-element.9.loss_i, f32[128,128]{1,0:T(8,128)S(1)} %get-tuple-element.10.head_i, bf16[128,1024]{1,0:T(8,128)(2,1)S(1)} %get-tuple-element.11.gh_i), custom_call_target="tpu_custom_call" | custom-call | tf_op jit(solution)/shard_map/write_out/pallas_call | solution.py:397
where the time goes:
time: 26 us; the launch traced here: 25.9 us
  Pallas kernels  25.2 us (97%)
  between operations  0.64 us (2%)
    pallas_call x1, Pallas kernels, per_device_kernel(): pl.pallas_call(functools.partial(kernel, (DP, T, S)), out_shape=shapes, i...  23.9 us
    pallas_call x1, Pallas kernels, per_device_kernel(): pl.pallas_call(write_out, out_shape=shapes, in_specs=[pl.BlockSpec(memory...  1.38 us

commit v1 on v0

v1 whole, which is shorter than its diff:
```python
import functools

import jax
import jax.numpy as jnp
from jax import lax
from jax.experimental import pallas as pl
from jax.experimental.pallas import tpu as pltpu
from jax.sharding import PartitionSpec as P

F32 = jnp.float32
BF16 = jnp.bfloat16
MESH = pl.DeviceIdType.MESH
KCH = 2
GCAT = 3


def decode_terms(context, tok_rows, mask_rows, embed, gain, w_head, count_fn):
    frames = context.shape[0]
    width = context.shape[1]
    steps = tok_rows.shape[1]
    before = embed[tok_rows[:, :-1]].astype(jnp.float32)
    leading = jnp.zeros((frames, 1, width), jnp.float32)
    inputs = context.astype(jnp.float32)[:, None, :] + jnp.concatenate([leading, before], 1)
    inverse = lax.rsqrt(jnp.mean(inputs * inputs, -1, keepdims=True) + 1e-06)
    normed = inputs * inverse
    scaled = (normed * gain).astype(jnp.bfloat16)
    flat = scaled.reshape(frames * steps, width)
    logits = jnp.dot(flat, w_head, preferred_element_type=jnp.float32)
    top = jnp.max(logits, -1, keepdims=True)
    total = top[:, 0] + jnp.log(jnp.sum(jnp.exp(logits - top), -1))
    target = tok_rows.reshape(-1)
    onehot = (target[:, None] == jnp.arange(w_head.shape[1], dtype=jnp.int32)[None, :]).astype(
        jnp.float32
    )
    nll = total - jnp.sum(logits * onehot, -1)
    weights = (mask_rows.astype(jnp.float32)[:, None] * jnp.ones((1, steps), jnp.float32)).reshape(
        -1
    )
    count, loss_sum = count_fn(
        steps * jnp.sum(mask_rows.astype(jnp.float32)), jnp.sum(weights * nll)
    )
    probs = jnp.exp(logits - total[:, None])
    grad_logits = ((probs - onehot) * weights[:, None] / count).astype(jnp.bfloat16)
    head_term = lax.dot_general(
        flat, grad_logits, (((0,), (0,)), ((), ())), preferred_element_type=jnp.float32
    )
    grad_scaled = lax.dot_general(
        grad_logits, w_head, (((1,), (1,)), ((), ())), preferred_element_type=jnp.float32
    )
    scaled_grad = grad_scaled.reshape(inputs.shape) * gain
    grad_inputs = inverse * (
        scaled_grad - normed * jnp.mean(scaled_grad * normed, -1, keepdims=True)
    )
    grad_context = jnp.sum(grad_inputs, 1).astype(jnp.bfloat16)
    return (loss_sum / count, head_term, grad_context)


def add_totals(count_local, loss_local):
    return lax.psum((count_local, loss_local), ("dp", "tensor", "seq"))


def per_device_plain(hidden, w_in, embed, gain, w_head, tokens, frame_mask):
    groups = lax.axis_size("tensor")
    rows = hidden.shape[0] // groups
    context = lax.psum_scatter(
        jnp.dot(hidden, w_in, preferred_element_type=jnp.float32),
        "tensor",
        scatter_dimension=0,
        tiled=True,
    ).astype(jnp.bfloat16)
    offset = lax.axis_index("tensor") * rows
    tok_rows = lax.dynamic_slice_in_dim(tokens, offset, rows, 0)
    mask_rows = lax.dynamic_slice_in_dim(frame_mask, offset, rows, 0)
    loss, head_term, grad_context = decode_terms(
        context, tok_rows, mask_rows, embed, gain, w_head, add_totals
    )
    flat_term = head_term.reshape(-1)
    partial_grad = lax.psum_scatter(
        flat_term.astype(jnp.bfloat16), "dp", scatter_dimension=0, tiled=True
    ).astype(jnp.float32)
    grad_head = lax.psum_scatter(partial_grad, ("tensor", "seq"), scatter_dimension=0, tiled=True)
    product = lax.dot_general(
        lax.all_gather(grad_context, "tensor", axis=0, tiled=True),
        w_in,
        (((1,), (1,)), ((), ())),
        preferred_element_type=jnp.float32,
    )
    grad_hidden = product.astype(jnp.bfloat16)
    return (loss, grad_head, grad_hidden)


def kernel(
    sizes, hidden_h, w_in_h, embed_h, gain_h, w_head_h, tokens_h, mask_h,
    loss_o, head_o, gh_o,
    hidden, w_in, embed, gain, w_head, tokens, mask,
    ctx_own, ctx_send, ctx_recv, gath, scaled, gl, hs, r1, s1, r2, s2, r3, own,
    gc, st1, st1_r, st2, st2_r,
    in_sem, ctx_ss, ctx_rs, gc_ss, gc_rs,
    h1_ss, h1_rs, h2_ss, h2_rs, h3_ss, h3_rs, st1_ss, st1_rs, st2_ss, st2_rs,
):
    DP, T, S = sizes
    a, t, s = lax.axis_index("dp"), lax.axis_index("tensor"), lax.axis_index("seq")
    steps, nframes = tokens.shape
    frames = nframes // T
    feats = hidden.shape[1]
    width, vocab = w_head.shape
    rows = frames * steps
    piece = width // (DP * T * S)

    TX = 2 if T % 2 == 0 else 1
    TY = T // TX
    ty, tx = t // TX, lax.rem(t, TX)
    moves = sorted(
        [(dy, dx) for dy in range(TY) for dx in range(TX) if dy or dx],
        key=lambda m: -(m[0] > 0) - (m[1] > 0),
    )
    places = [lax.rem(ty + dy, TY) * TX + lax.rem(tx + dx, TX) for dy, dx in moves]

    barrier = pltpu.get_barrier_semaphore()
    peers_t = [{"tensor": p} for p in places]
    peers_p = [
        {"tensor": lax.rem(t + d, T), "seq": lax.rem(s + e, S)}
        for d in range(T)
        for e in range(S)
        if d or e
    ]
    peers_d = [{"dp": lax.rem(a + d, DP)} for d in range(1, DP)]
    for peer in peers_d + peers_p:
        pl.semaphore_signal(barrier, inc=1, device_id=peer, device_id_type=MESH)

    K = KCH
    part_k = feats // K
    pairs = []
    for i in range(K):
        at = pl.ds(i * part_k, part_k)
        pairs.append((hidden_h.at[:, at], hidden.at[:, at]))
        pairs.append((w_in_h.at[at, :], w_in.at[at, :]))
    pairs += [
        (tokens_h, tokens),
        (mask_h, mask),
        (embed_h, embed),
        (gain_h, gain),
        (w_head_h, w_head),
    ]
    loads = [
        pltpu.make_async_copy(src, dst, in_sem.at[i]) for i, (src, dst) in enumerate(pairs)
    ]
    for load in loads:
        load.start()
    rest = loads[2 * K :]

    sends = []

    def got(copy):
        copy.wait_recv()

    def send(src, dst, ss, rs, peer):
        copy = pltpu.make_async_remote_copy(
            src_ref=src, dst_ref=dst, send_sem=ss, recv_sem=rs, device_id=peer, device_id_type=MESH
        )
        copy.start()
        sends.append(copy)
        return copy

    part = None
    for i in range(K):
        loads[2 * i].wait()
        loads[2 * i + 1].wait()
        at = pl.ds(i * part_k, part_k)
        more = jnp.dot(hidden[:, at], w_in[at, :], preferred_element_type=F32)
        part = more if part is None else part + more
    part = part.reshape(T, frames, width)
    ctx_send[...] = part.astype(BF16)
    ctx_own[...] = part
    pl.semaphore_wait(barrier, len(peers_d) + len(peers_p))
    ctx_copies = [
        send(ctx_send.at[p], ctx_recv.at[i], ctx_ss.at[i], ctx_rs.at[i], peers_t[i])
        for i, p in enumerate(places)
    ]

    rest[0].wait()
    rest[1].wait()
    mask_row = mask[...].astype(F32)
    spot = lax.broadcasted_iota(jnp.int32, (frames, nframes), 0) + t * frames
    here = lax.broadcasted_iota(jnp.int32, (frames, nframes), 1)
    mine = spot == here
    tok = tokens[...].astype(F32)
    lanes = lax.broadcasted_iota(jnp.int32, (frames, vocab), 1).astype(F32)
    hot = [
        jnp.sum(jnp.where(mine, tok[k : k + 1, :], 0.0), 1, keepdims=True) == lanes
        for k in range(steps)
    ]
    rest[2].wait()
    prev = jnp.concatenate([jnp.where(h, 1.0, 0.0).astype(BF16) for h in hot[:-1]], 0)
    gath[...] = jnp.dot(prev, embed[...], preferred_element_type=F32)
    mcol = jnp.sum(jnp.where(mine, mask_row, 0.0), 1, keepdims=True)
    rest[3].wait()
    rest[4].wait()
    gvec = gain[...]

    ctx = ctx_own[t]
    for i in range(T - 1):
        got(ctx_copies[i])
        ctx = ctx + ctx_recv[i].astype(F32)
    ctx = ctx.astype(BF16).astype(F32)
    inputs = jnp.concatenate([ctx] * steps, 0) + jnp.concatenate(
        [jnp.zeros((frames, width), F32), gath[...]], 0
    )
    inverse = lax.rsqrt(jnp.mean(inputs * inputs, -1, keepdims=True) + 1e-06)
    normed = inputs * inverse
    flat = (normed * gvec).astype(BF16)
    scaled[...] = flat
    logits = jnp.dot(flat, w_head[...], preferred_element_type=F32)
    top = jnp.max(logits, -1, keepdims=True)
    powers = jnp.exp(logits - top)
    norm = jnp.sum(powers, -1, keepdims=True)
    onehot = jnp.concatenate([jnp.where(h, 1.0, 0.0) for h in hot], 0)
    weights = jnp.concatenate([mcol] * steps, 0)
    grads = ((powers * (1.0 / norm) - onehot) * weights).astype(BF16)
    gl[...] = grads

    chunk = width // DP
    h1, h2 = [], []

    def tensor_stage(j):
        acc = hs[j, :, s].astype(F32)
        for e in range(1, S):
            got(h1[j * (S - 1) + e - 1])
            acc = acc + r1[j, e - 1].astype(F32)
        s1[j] = acc.astype(BF16)
        for i, p in enumerate(places):
            h2.append(
                send(s1.at[j, p], r2.at[j, i], h2_ss.at[j, i], h2_rs.at[j, i], peers_t[i])
            )

    for j in range(DP):
        term = lax.dot_general(
            scaled[:, j * chunk : (j + 1) * chunk], gl[...], (((0,), (0,)), ((), ())),
            preferred_element_type=F32,
        )
        hs[j] = term.astype(BF16).reshape(T, S, piece, vocab)
        for e in range(1, S):
            h1.append(
                send(hs.at[j, :, lax.rem(s + e, S)], r1.at[j, e - 1], h1_ss.at[j, e - 1],
                     h1_rs.at[j, e - 1], {"seq": lax.rem(s + e, S)})
            )

    total = top + jnp.log(norm)
    nll = total - jnp.sum(logits * onehot, -1, keepdims=True)
    left = lax.broadcasted_iota(jnp.int32, st1.shape, 1) < st1.shape[1] // 2
    st1[...] = jnp.where(left, jnp.sum(weights * nll), jnp.sum(weights))
    stat1 = [
        send(st1, st1_r.at[i], st1_ss.at[i], st1_rs.at[i], peer) for i, peer in enumerate(peers_p)
    ]

    gc_copies = []

    def context_grad():
        grad_scaled = lax.dot_general(
            gl[...], w_head[...], (((1,), (1,)), ((), ())), preferred_element_type=F32
        )
        g = grad_scaled * gvec
        gi = inverse * (g - normed * jnp.mean(g * normed, -1, keepdims=True))
        gsum = gi[0:frames]
        for k in range(1, steps):
            gsum = gsum + gi[k * frames : (k + 1) * frames]
        gc[t] = gsum.astype(BF16)
        for i in range(T - 1):
            gc_copies.append(
                send(gc.at[t], gc.at[t], gc_ss.at[i], gc_rs.at[i], peers_t[i])
            )

    for j in range(DP):
        tensor_stage(j)
        if j == min(GCAT, DP - 1):
            context_grad()

    stats = st1[...]
    for i in range(len(peers_p)):
        got(stat1[i])
        stats = stats + st1_r[i]
    st2[...] = stats
    stat2 = [
        send(st2, st2_r.at[i], st2_ss.at[i], st2_rs.at[i], peer) for i, peer in enumerate(peers_d)
    ]

    def passes(j, slot, src):
        return pltpu.make_async_remote_copy(
            src_ref=src, dst_ref=r3.at[slot], send_sem=h3_ss.at[j], recv_sem=h3_rs.at[slot],
            device_id={"dp": j}, device_id_type=MESH,
        )

    for j in range(DP):
        acc = s1[j, t].astype(F32)
        for i in range(T - 1):
            got(h2[j * (T - 1) + i])
            acc = acc + r2[j, i].astype(F32)

        @pl.when(a == j)
        def _():
            own[...] = acc

        @pl.when(a != j)
        def _():
            s2[j] = acc.astype(BF16)
            passes(j, lax.rem(j - a + DP, DP) - 1, s2.at[j]).start()

    for i in range(DP - 1):
        got(stat2[i])
        stats = stats + st2_r[i]
    half = st1.shape[1] // 2
    share = 1.0 / stats[0:1, half : half + 1]
    for i in range(T - 1):
        got(gc_copies[i])
    product = lax.dot_general(
        gc[...].reshape(nframes, width), w_in[...], (((1,), (1,)), ((), ())),
        preferred_element_type=F32,
    )
    gh_o[...] = (product * share).astype(BF16)
    loss_o[...] = stats * share

    acc = own[...]
    for d in range(DP - 1):
        pltpu.make_async_remote_copy(
            src_ref=s2.at[d], dst_ref=r3.at[d], send_sem=h3_ss.at[d], recv_sem=h3_rs.at[d],
            device_id={"dp": lax.rem(a + 1, DP)}, device_id_type=MESH,
        ).wait_recv()
        acc = acc + r3[d].astype(F32)
    acc = acc * share
    groups = vocab // 128
    for b in range(groups):
        head_o[pl.ds(b, piece, stride=groups), :] = acc[:, b * 128 : (b + 1) * 128]
    for copy in sends:
        copy.wait_send()
    for j in range(DP):

        @pl.when(a != j)
        def _():
            passes(j, 0, s2.at[j]).wait_send()


def write_out(loss_i, head_i, gh_i, loss_o, head_o, gh_o, loss_v, sem):
    copies = [
        pltpu.make_async_copy(src, dst, sem.at[i])
        for i, (src, dst) in enumerate([(gh_i, gh_o), (head_i, head_o), (loss_v, loss_o)])
    ]
    copies[0].start()
    copies[1].start()
    loss_v[...] = loss_i[0:1, 0:1]
    copies[2].start()
    for copy in copies:
        copy.wait()


def per_device_kernel(hidden, w_in, embed, gain, w_head, tokens, frame_mask):
    DP, T, S = lax.axis_size("dp"), lax.axis_size("tensor"), lax.axis_size("seq")
    nframes, feats = hidden.shape
    steps = tokens.shape[1]
    frames = nframes // T
    width, vocab = w_head.shape
    rows = frames * steps
    piece = width // (DP * T * S)
    V = pltpu.VMEM
    dma = pltpu.SemaphoreType.DMA
    scratch = [
        V(hidden.shape, BF16), V(w_in.shape, BF16), V(embed.shape, BF16), V((1, width), F32),
        V(w_head.shape, BF16), V((steps, nframes), jnp.int32), V((1, nframes), jnp.int32),
        V((T, frames, width), F32),
        V((T, frames, width), BF16),
        V((T - 1, frames, width), BF16),
        V((rows - frames, width), F32),
        V((rows, width), BF16),
        V((rows, vocab), BF16),
        V((DP, T, S, piece, vocab), BF16),
        V((DP, S - 1, T, piece, vocab), BF16),
        V((DP, T, piece, vocab), BF16),
        V((DP, T - 1, piece, vocab), BF16),
        V((DP, piece, vocab), BF16),
        V((DP - 1, piece, vocab), BF16),
        V((piece, vocab), F32),
        V((T, frames, width), BF16),
        V((8, 128), F32), V((T * S - 1, 8, 128), F32),
        V((8, 128), F32), V((DP - 1, 8, 128), F32),
        dma((2 * KCH + 5,)),
        dma((T - 1,)), dma((T - 1,)), dma((T - 1,)), dma((T - 1,)),
        dma((DP, S - 1)), dma((DP, S - 1)), dma((DP, T - 1)), dma((DP, T - 1)),
        dma((DP,)), dma((DP - 1,)),
        dma((T * S - 1,)), dma((T * S - 1,)), dma((DP - 1,)), dma((DP - 1,)),
    ]
    head_shape = jax.ShapeDtypeStruct((piece * vocab // 128, 128), F32)
    gh_shape = jax.ShapeDtypeStruct((nframes, feats), BF16)
    vmem = pl.BlockSpec(memory_space=pltpu.VMEM)
    results = pl.pallas_call(
        functools.partial(kernel, (DP, T, S)),
        out_shape=(jax.ShapeDtypeStruct((8, 128), F32), head_shape, gh_shape),
        in_specs=[pl.BlockSpec(memory_space=pltpu.HBM)] * 7,
        out_specs=(vmem, vmem, vmem),
        scratch_shapes=scratch,
        compiler_params=pltpu.CompilerParams(
            collective_id=0, has_side_effects=True, vmem_limit_bytes=40 << 20
        ),
        name="decode",
    )(*[pltpu.with_memory_space_constraint(x, pltpu.HBM) for x in (hidden, w_in, embed, gain.reshape(1, -1), w_head, tokens.T, frame_mask.reshape(1, -1))])
    loss, head, grad_hidden = pl.pallas_call(
        write_out,
        out_shape=(jax.ShapeDtypeStruct((1, 1), F32), head_shape, gh_shape),
        in_specs=[vmem] + [pl.BlockSpec(memory_space=pl.ANY)] * 2,
        out_specs=(pl.BlockSpec(memory_space=pltpu.HBM),) * 3,
        scratch_shapes=[V((1, 1), F32), dma((3,))],
        compiler_params=pltpu.CompilerParams(vmem_limit_bytes=4 << 20),
        name="write_out",
    )(*results)
    return loss.reshape(()), head.reshape(-1), grad_hidden


def solution(mesh):
    def per_device(hidden, w_in, embed, gain, w_head, tokens, frame_mask):
        DP, T, S = mesh.shape["dp"], mesh.shape["tensor"], mesh.shape["seq"]
        width, vocab = w_head.shape
        fits = (
            width % (16 * DP * T * S) == 0
            and width % (128 * DP) == 0
            and vocab % 128 == 0
            and hidden.shape[0] % (16 * T) == 0
            and min(DP, T, S) > 1
        )
        run = per_device_kernel if fits else per_device_plain
        return run(hidden, w_in, embed, gain, w_head, tokens, frame_mask)

    placed = (
        P(("dp", "seq"), "tensor"),
        P("tensor", None),
        P(),
        P(),
        P(),
        P(("dp", "seq"), None),
        P(("dp", "seq")),
    )
    return jax.shard_map(
        per_device,
        mesh=mesh,
        in_specs=placed,
        out_specs=(P(), P(("dp", "tensor", "seq")), P(("dp", "seq"), "tensor")),
        check_vma=False,
    )
```

time: 26 us -> 23.8 us (0.915)
  Pallas kernels: 25.2 us -> 23 us
    pallas_call x2, Pallas kernels: 25.2 us -> 23 us  [the longest x1 22.3 us: per_device_kernel(): pl.pallas_call(functools.partial(kernel, (DP, T, S)), out_shape=(jax.Shap...]
where the time goes in v1:
time: 23.8 us; the launch traced here: 23.7 us
  Pallas kernels  23 us (97%)
  between operations  0.64 us (3%)
    pallas_call x1, Pallas kernels, per_device_kernel(): pl.pallas_call(functools.partial(kernel, (DP, T, S)), out_shape=(jax.Shap...  22.3 us
    pallas_call x1, Pallas kernels, per_device_kernel(): pl.pallas_call(write_out, out_shape=(jax.ShapeDtypeStruct((1, 1), F32), h...  0.75 us

profile of v1, /device:TPU:0, one launch (start us, length us, event | category | flops | bytes accessed | tf_op | source)
XLA Modules:
  0.0 23.7 jit_solution(13449667363352846417)
XLA Ops:
  0.6 22.3 %decode.1 = (f32[8,128]{1,0:T(8,128)S(1)}, f32[128,128]{1,0:T(8,128)S(1)}, bf16[128,1024]{1,0:T(8,128)(2,1)S(1)}) custom-call(bf16[128,1024]{1,0:T(8,128)(2,1)} %hidden_h.1, bf16[1024,512]{1,0:T(8,128)(2,1)} %w_in_h.1, bf16[1024,512]{1,0:T(8,128)(2,1)} %embed_h.1, f32[1,512]{1,0:T(1,128)} %bitcast.6, bf16[512,1024]{1,0:T(8,128)(2,1)} %w_head_h.1, ...), custom_call_target="tpu_custom_call" | custom-call | tf_op jit(solution)/shard_map/decode/pallas_call | solution.py:393
  22.9 0.7 %write_out.1 = (f32[1,1]{1,0:T(1,128)}, f32[128,128]{1,0:T(8,128)}, bf16[128,1024]{1,0:T(8,128)(2,1)}) custom-call(f32[8,128]{1,0:T(8,128)S(1)} %get-tuple-element.9.loss_i, f32[128,128]{1,0:T(8,128)S(1)} %get-tuple-element.10.head_i, bf16[128,1024]{1,0:T(8,128)(2,1)S(1)} %get-tuple-element.11.gh_i), custom_call_target="tpu_custom_call" | custom-call | tf_op jit(solution)/shard_map/write_out/pallas_call | solution.py:404

commit v2 on v1

--- a/solution.py
+++ b/solution.py
@@ -11,7 +11,13 @@
 BF16 = jnp.bfloat16
 MESH = pl.DeviceIdType.MESH
 KCH = 2
+PAIR = 2
 GCAT = 3
+STAT = -1
+LAT = 0
+EARLY = 2
+ZAT = 2
+ZSHARE = 3
 
 
 def decode_terms(context, tok_rows, mask_rows, embed, gain, w_head, count_fn):
@@ -94,9 +100,10 @@
     loss_o, head_o, gh_o,
     hidden, w_in, embed, gain, w_head, tokens, mask,
     ctx_own, ctx_send, ctx_recv, gath, scaled, gl, hs, r1, s1, r2, s2, r3, own,
-    gc, st1, st1_r, st2, st2_r,
+    z1, rz, zown, z2, rz2, gc, st1, st1_r, st2, st2_r,
     in_sem, ctx_ss, ctx_rs, gc_ss, gc_rs,
-    h1_ss, h1_rs, h2_ss, h2_rs, h3_ss, h3_rs, st1_ss, st1_rs, st2_ss, st2_rs,
+    h1_ss, h1_rs, h2_ss, h2_rs, h3_ss, h3_rs, z1_ss, z1_rs, z2_ss, z2_rs,
+    st1_ss, st1_rs, st2_ss, st2_rs,
 ):
     DP, T, S = sizes
     a, t, s = lax.axis_index("dp"), lax.axis_index("tensor"), lax.axis_index("seq")
@@ -145,9 +152,9 @@
     loads = [
         pltpu.make_async_copy(src, dst, in_sem.at[i]) for i, (src, dst) in enumerate(pairs)
     ]
-    for load in loads:
+    rest = loads[2 * K :]
+    for load in loads[: 2 * K] + rest[:EARLY]:
         load.start()
-    rest = loads[2 * K :]
 
     sends = []
 
@@ -169,6 +176,9 @@
         at = pl.ds(i * part_k, part_k)
         more = jnp.dot(hidden[:, at], w_in[at, :], preferred_element_type=F32)
         part = more if part is None else part + more
+        if i == 0:
+            for load in rest[EARLY:]:
+                load.start()
     part = part.reshape(T, frames, width)
     ctx_send[...] = part.astype(BF16)
     ctx_own[...] = part
@@ -222,36 +232,55 @@
     chunk = width // DP
     h1, h2 = [], []
 
+    cut = s1.shape[3]
+
+    def along_dp(j, slot, src, dst, ss, rs):
+        return pltpu.make_async_remote_copy(
+            src_ref=src, dst_ref=dst.at[slot], send_sem=ss.at[j], recv_sem=rs.at[slot],
+            device_id={"dp": j}, device_id_type=MESH,
+        )
+
     def tensor_stage(j):
         acc = hs[j, :, s].astype(F32)
         for e in range(1, S):
             got(h1[j * (S - 1) + e - 1])
             acc = acc + r1[j, e - 1].astype(F32)
-        s1[j] = acc.astype(BF16)
+        s1[j] = acc[:, :, :cut].astype(BF16)
         for i, p in enumerate(places):
             h2.append(
                 send(s1.at[j, p], r2.at[j, i], h2_ss.at[j, i], h2_rs.at[j, i], peers_t[i])
             )
 
-    for j in range(DP):
+        z1[j] = acc[:, :, cut:].astype(BF16)
+
+        @pl.when(a != j)
+        def _():
+            along_dp(j, lax.rem(j - a + DP, DP) - 1, z1.at[j], rz, z1_ss, z1_rs).start()
+
+    for j0 in range(0, DP, PAIR):
         term = lax.dot_general(
-            scaled[:, j * chunk : (j + 1) * chunk], gl[...], (((0,), (0,)), ((), ())),
+            scaled[:, j0 * chunk : (j0 + PAIR) * chunk], gl[...], (((0,), (0,)), ((), ())),
             preferred_element_type=F32,
         )
-        hs[j] = term.astype(BF16).reshape(T, S, piece, vocab)
-        for e in range(1, S):
-            h1.append(
-                send(hs.at[j, :, lax.rem(s + e, S)], r1.at[j, e - 1], h1_ss.at[j, e - 1],
-                     h1_rs.at[j, e - 1], {"seq": lax.rem(s + e, S)})
+        for j in range(j0, j0 + PAIR):
+            hs[j] = term[(j - j0) * chunk : (j - j0 + 1) * chunk].astype(BF16).reshape(
+                T, S, piece, vocab
             )
-
-    total = top + jnp.log(norm)
-    nll = total - jnp.sum(logits * onehot, -1, keepdims=True)
-    left = lax.broadcasted_iota(jnp.int32, st1.shape, 1) < st1.shape[1] // 2
-    st1[...] = jnp.where(left, jnp.sum(weights * nll), jnp.sum(weights))
-    stat1 = [
-        send(st1, st1_r.at[i], st1_ss.at[i], st1_rs.at[i], peer) for i, peer in enumerate(peers_p)
-    ]
+            for e in range(1, S):
+                h1.append(
+                    send(hs.at[j, :, lax.rem(s + e, S)], r1.at[j, e - 1], h1_ss.at[j, e - 1],
+                         h1_rs.at[j, e - 1], {"seq": lax.rem(s + e, S)})
+                )
+
+    stat1, stat2 = [], []
+
+    def statistics():
+        total = top + jnp.log(norm)
+        nll = total - jnp.sum(logits * onehot, -1, keepdims=True)
+        left = lax.broadcasted_iota(jnp.int32, st1.shape, 1) < st1.shape[1] // 2
+        st1[...] = jnp.where(left, jnp.sum(weights * nll), jnp.sum(weights))
+        for i, peer in enumerate(peers_p):
+            stat1.append(send(st1, st1_r.at[i], st1_ss.at[i], st1_rs.at[i], peer))
 
     gc_copies = []
 
@@ -270,27 +299,38 @@
                 send(gc.at[t], gc.at[t], gc_ss.at[i], gc_rs.at[i], peers_t[i])
             )
 
+    if STAT < 0:
+        statistics()
     for j in range(DP):
         tensor_stage(j)
+        if j == min(STAT, DP - 1):
+            statistics()
         if j == min(GCAT, DP - 1):
             context_grad()
 
-    stats = st1[...]
-    for i in range(len(peers_p)):
-        got(stat1[i])
-        stats = stats + st1_r[i]
-    st2[...] = stats
-    stat2 = [
-        send(st2, st2_r.at[i], st2_ss.at[i], st2_rs.at[i], peer) for i, peer in enumerate(peers_d)
-    ]
-
-    def passes(j, slot, src):
-        return pltpu.make_async_remote_copy(
-            src_ref=src, dst_ref=r3.at[slot], send_sem=h3_ss.at[j], recv_sem=h3_rs.at[slot],
-            device_id={"dp": j}, device_id_type=MESH,
-        )
+    z2c = []
+
+    def z_stage():
+        acc = jnp.zeros(zown.shape, F32)
+        for j in range(DP):
+            acc = acc + jnp.where(a == j, z1[j].astype(F32), 0.0)
+        for d in range(DP - 1):
+            along_dp(d, d, z1.at[d], rz, z1_ss, z1_rs).wait_recv()
+            acc = acc + rz[d].astype(F32)
+        z2[...] = acc.astype(BF16)
+        zown[...] = acc
+        for i, p in enumerate(places):
+            z2c.append(send(z2.at[p], rz2.at[i], z2_ss.at[i], z2_rs.at[i], peers_t[i]))
 
     for j in range(DP):
+        if j == min(LAT, DP - 1):
+            stats = st1[...]
+            for i in range(len(peers_p)):
+                got(stat1[i])
+                stats = stats + st1_r[i]
+            st2[...] = stats
+            for i, peer in enumerate(peers_d):
+                stat2.append(send(st2, st2_r.at[i], st2_ss.at[i], st2_rs.at[i], peer))
         acc = s1[j, t].astype(F32)
         for i in range(T - 1):
             got(h2[j * (T - 1) + i])
@@ -303,7 +343,10 @@
         @pl.when(a != j)
         def _():
             s2[j] = acc.astype(BF16)
-            passes(j, lax.rem(j - a + DP, DP) - 1, s2.at[j]).start()
+            along_dp(j, lax.rem(j - a + DP, DP) - 1, s2.at[j], r3, h3_ss, h3_rs).start()
+
+        if j == min(ZAT, DP - 1):
+            z_stage()
 
     for i in range(DP - 1):
         got(stat2[i])
@@ -319,16 +362,21 @@
     gh_o[...] = (product * share).astype(BF16)
     loss_o[...] = stats * share
 
+    groups = vocab // 128
+    low = cut // 128
+    acc = zown[t]
+    for i in range(T - 1):
+        got(z2c[i])
+        acc = acc + rz2[i].astype(F32)
+    acc = acc * share
+    for b in range(low, groups):
+        head_o[pl.ds(b, piece, stride=groups), :] = acc[:, (b - low) * 128 : (b - low + 1) * 128]
     acc = own[...]
     for d in range(DP - 1):
-        pltpu.make_async_remote_copy(
-            src_ref=s2.at[d], dst_ref=r3.at[d], send_sem=h3_ss.at[d], recv_sem=h3_rs.at[d],
-            device_id={"dp": lax.rem(a + 1, DP)}, device_id_type=MESH,
-        ).wait_recv()
+        along_dp(d, d, s2.at[d], r3, h3_ss, h3_rs).wait_recv()
         acc = acc + r3[d].astype(F32)
     acc = acc * share
-    groups = vocab // 128
-    for b in range(groups):
+    for b in range(low):
         head_o[pl.ds(b, piece, stride=groups), :] = acc[:, b * 128 : (b + 1) * 128]
     for copy in sends:
         copy.wait_send()
@@ -336,7 +384,8 @@
 
         @pl.when(a != j)
         def _():
-            passes(j, 0, s2.at[j]).wait_send()
+            along_dp(j, 0, z1.at[j], rz, z1_ss, z1_rs).wait_send()
+            along_dp(j, 0, s2.at[j], r3, h3_ss, h3_rs).wait_send()
 
 
 def write_out(loss_i, head_i, gh_i, loss_o, head_o, gh_o, loss_v, sem):
@@ -360,6 +409,8 @@
     width, vocab = w_head.shape
     rows = frames * steps
     piece = width // (DP * T * S)
+    tail = max(vocab // 128 * ZSHARE // 8, 1) * 128
+    cut = vocab - tail
     V = pltpu.VMEM
     dma = pltpu.SemaphoreType.DMA
     scratch = [
@@ -373,18 +424,23 @@
         V((rows, vocab), BF16),
         V((DP, T, S, piece, vocab), BF16),
         V((DP, S - 1, T, piece, vocab), BF16),
-        V((DP, T, piece, vocab), BF16),
-        V((DP, T - 1, piece, vocab), BF16),
-        V((DP, piece, vocab), BF16),
-        V((DP - 1, piece, vocab), BF16),
-        V((piece, vocab), F32),
+        V((DP, T, piece, cut), BF16),
+        V((DP, T - 1, piece, cut), BF16),
+        V((DP, piece, cut), BF16),
+        V((DP - 1, piece, cut), BF16),
+        V((piece, cut), F32),
+        V((DP, T, piece, tail), BF16),
+        V((DP - 1, T, piece, tail), BF16),
+        V((T, piece, tail), F32),
+        V((T, piece, tail), BF16),
+        V((T - 1, piece, tail), BF16),
         V((T, frames, width), BF16),
         V((8, 128), F32), V((T * S - 1, 8, 128), F32),
         V((8, 128), F32), V((DP - 1, 8, 128), F32),
         dma((2 * KCH + 5,)),
         dma((T - 1,)), dma((T - 1,)), dma((T - 1,)), dma((T - 1,)),
         dma((DP, S - 1)), dma((DP, S - 1)), dma((DP, T - 1)), dma((DP, T - 1)),
-        dma((DP,)), dma((DP - 1,)),
+        dma((DP,)), dma((DP - 1,)), dma((DP,)), dma((DP - 1,)), dma((T - 1,)), dma((T - 1,)),
         dma((T * S - 1,)), dma((T * S - 1,)), dma((DP - 1,)), dma((DP - 1,)),
     ]
     head_shape = jax.ShapeDtypeStruct((piece * vocab // 128, 128), F32)
@@ -421,8 +477,10 @@
             width % (16 * DP * T * S) == 0
             and width % (128 * DP) == 0
             and vocab % 128 == 0
+            and vocab > 128
             and hidden.shape[0] % (16 * T) == 0
             and min(DP, T, S) > 1
+            and DP % PAIR == 0
         )
         run = per_device_kernel if fits else per_device_plain
         return run(hidden, w_in, embed, gain, w_head, tokens, frame_mask)

time: 23.8 us -> 21.7 us (0.912)
  Pallas kernels: 23 us -> 20.9 us
    pallas_call x1, Pallas kernels: 22.3 us -> 20.2 us  [per_device_kernel(): pl.pallas_call(functools.partial(kernel, (DP, T, S)), out_shape=(jax.Shap...]
where the time goes in v2:
time: 21.7 us; the launch traced here: 21.6 us
  Pallas kernels  20.9 us (96%)
  between operations  0.64 us (3%)
    pallas_call x1, Pallas kernels, per_device_kernel(): pl.pallas_call(functools.partial(kernel, (DP, T, S)), out_shape=(jax.Shap...  20.2 us
    pallas_call x1, Pallas kernels, per_device_kernel(): pl.pallas_call(write_out, out_shape=(jax.ShapeDtypeStruct((1, 1), F32), h...  0.75 us

profile of v2, /device:TPU:0, one launch (start us, length us, event | category | flops | bytes accessed | tf_op | source)
XLA Modules:
  0.0 21.6 jit_solution(4260723816843387140)
XLA Ops:
  0.6 20.2 %decode.1 = (f32[8,128]{1,0:T(8,128)S(1)}, f32[128,128]{1,0:T(8,128)S(1)}, bf16[128,1024]{1,0:T(8,128)(2,1)S(1)}) custom-call(bf16[128,1024]{1,0:T(8,128)(2,1)} %hidden_h.1, bf16[1024,512]{1,0:T(8,128)(2,1)} %w_in_h.1, bf16[1024,512]{1,0:T(8,128)(2,1)} %embed_h.1, f32[1,512]{1,0:T(1,128)} %bitcast.6, bf16[512,1024]{1,0:T(8,128)(2,1)} %w_head_h.1, ...), custom_call_target="tpu_custom_call" | custom-call | tf_op jit(solution)/shard_map/decode/pallas_call | solution.py:449
  20.8 0.7 %write_out.1 = (f32[1,1]{1,0:T(1,128)}, f32[128,128]{1,0:T(8,128)}, bf16[128,1024]{1,0:T(8,128)(2,1)}) custom-call(f32[8,128]{1,0:T(8,128)S(1)} %get-tuple-element.9.loss_i, f32[128,128]{1,0:T(8,128)S(1)} %get-tuple-element.10.head_i, bf16[128,1024]{1,0:T(8,128)(2,1)S(1)} %get-tuple-element.11.gh_i), custom_call_target="tpu_custom_call" | custom-call | tf_op jit(solution)/shard_map/write_out/pallas_call | solution.py:460

commit v3 on v2

--- a/solution.py
+++ b/solution.py
@@ -11,12 +11,12 @@
 BF16 = jnp.bfloat16
 MESH = pl.DeviceIdType.MESH
 KCH = 2
-PAIR = 2
+PAIR = 4
 GCAT = 3
 STAT = -1
 LAT = 0
-EARLY = 2
-ZAT = 2
+EARLY = 7
+ZAT = 1
 ZSHARE = 3
 
 

time: 21.7 us -> 21.1 us (0.972)
  Pallas kernels: 20.9 us -> 20.3 us
    pallas_call x1, Pallas kernels: 20.2 us -> 19.5 us  [per_device_kernel(): pl.pallas_call(functools.partial(kernel, (DP, T, S)), out_shape=(jax.Shap...]
where the time goes in v3:
time: 21.1 us; the launch traced here: 20.9 us
  Pallas kernels  20.3 us (96%)
  between operations  0.64 us (3%)
    pallas_call x1, Pallas kernels, per_device_kernel(): pl.pallas_call(functools.partial(kernel, (DP, T, S)), out_shape=(jax.Shap...  19.5 us
    pallas_call x1, Pallas kernels, per_device_kernel(): pl.pallas_call(write_out, out_shape=(jax.ShapeDtypeStruct((1, 1), F32), h...  0.75 us

profile of v3, /device:TPU:0, one launch (start us, length us, event | category | flops | bytes accessed | tf_op | source)
XLA Modules:
  0.0 20.9 jit_solution(4283019073769495050)
XLA Ops:
  0.6 19.5 %decode.1 = (f32[8,128]{1,0:T(8,128)S(1)}, f32[128,128]{1,0:T(8,128)S(1)}, bf16[128,1024]{1,0:T(8,128)(2,1)S(1)}) custom-call(bf16[128,1024]{1,0:T(8,128)(2,1)} %hidden_h.1, bf16[1024,512]{1,0:T(8,128)(2,1)} %w_in_h.1, bf16[1024,512]{1,0:T(8,128)(2,1)} %embed_h.1, f32[1,512]{1,0:T(1,128)} %bitcast.6, bf16[512,1024]{1,0:T(8,128)(2,1)} %w_head_h.1, ...), custom_call_target="tpu_custom_call" | custom-call | tf_op jit(solution)/shard_map/decode/pallas_call | solution.py:449
  20.2 0.7 %write_out.1 = (f32[1,1]{1,0:T(1,128)}, f32[128,128]{1,0:T(8,128)}, bf16[128,1024]{1,0:T(8,128)(2,1)}) custom-call(f32[8,128]{1,0:T(8,128)S(1)} %get-tuple-element.9.loss_i, f32[128,128]{1,0:T(8,128)S(1)} %get-tuple-element.10.head_i, bf16[128,1024]{1,0:T(8,128)(2,1)S(1)} %get-tuple-element.11.gh_i), custom_call_target="tpu_custom_call" | custom-call | tf_op jit(solution)/shard_map/write_out/pallas_call | solution.py:460

commit v4 on v3

--- a/solution.py
+++ b/solution.py
@@ -11,13 +11,9 @@
 BF16 = jnp.bfloat16
 MESH = pl.DeviceIdType.MESH
 KCH = 2
-PAIR = 4
-GCAT = 3
-STAT = -1
-LAT = 0
+ORDER = ("T0", "T1", "T2", "T3", "J", "L", "K0", "K1", "Z", "K2", "K3", "S", "M")
+ZSHARE = 2
 EARLY = 7
-ZAT = 1
-ZSHARE = 3
 
 
 def decode_terms(context, tok_rows, mask_rows, embed, gain, w_head, count_fn):
@@ -103,13 +99,12 @@
     z1, rz, zown, z2, rz2, gc, st1, st1_r, st2, st2_r,
     in_sem, ctx_ss, ctx_rs, gc_ss, gc_rs,
     h1_ss, h1_rs, h2_ss, h2_rs, h3_ss, h3_rs, z1_ss, z1_rs, z2_ss, z2_rs,
-    st1_ss, st1_rs, st2_ss, st2_rs,
+    st1_ss, st1_rs, st2_ss, st2_rs, above, below,
 ):
     DP, T, S = sizes
     a, t, s = lax.axis_index("dp"), lax.axis_index("tensor"), lax.axis_index("seq")
     steps, nframes = tokens.shape
     frames = nframes // T
-    feats = hidden.shape[1]
     width, vocab = w_head.shape
     rows = frames * steps
     piece = width // (DP * T * S)
@@ -132,16 +127,24 @@
         if d or e
     ]
     peers_d = [{"dp": lax.rem(a + d, DP)} for d in range(1, DP)]
-    for peer in peers_d + peers_p:
+    for peer in peers_p:
         pl.semaphore_signal(barrier, inc=1, device_id=peer, device_id_type=MESH)
 
+    @pl.when(a > 0)
+    def _():
+        pl.semaphore_signal(barrier, inc=1, device_id={"dp": a - 1}, device_id_type=MESH)
+
+    @pl.when(a < DP - 1)
+    def _():
+        pl.semaphore_signal(barrier, inc=1, device_id={"dp": a + 1}, device_id_type=MESH)
+
+
     K = KCH
-    part_k = feats // K
-    pairs = []
+    part_n = width // K
+    pairs = [(hidden_h, hidden)]
     for i in range(K):
-        at = pl.ds(i * part_k, part_k)
-        pairs.append((hidden_h.at[:, at], hidden.at[:, at]))
-        pairs.append((w_in_h.at[at, :], w_in.at[at, :]))
+        at = pl.ds(i * part_n, part_n)
+        pairs.append((w_in_h.at[:, at], w_in.at[:, at]))
     pairs += [
         (tokens_h, tokens),
         (mask_h, mask),
@@ -152,8 +155,8 @@
     loads = [
         pltpu.make_async_copy(src, dst, in_sem.at[i]) for i, (src, dst) in enumerate(pairs)
     ]
-    rest = loads[2 * K :]
-    for load in loads[: 2 * K] + rest[:EARLY]:
+    rest = loads[K + 1 :]
+    for load in loads[: K + 1] + rest[:EARLY]:
         load.start()
 
     sends = []
@@ -169,24 +172,23 @@
         sends.append(copy)
         return copy
 
-    part = None
-    for i in range(K):
-        loads[2 * i].wait()
-        loads[2 * i + 1].wait()
-        at = pl.ds(i * part_k, part_k)
-        more = jnp.dot(hidden[:, at], w_in[at, :], preferred_element_type=F32)
-        part = more if part is None else part + more
-        if i == 0:
-            for load in rest[EARLY:]:
-                load.start()
-    part = part.reshape(T, frames, width)
-    ctx_send[...] = part.astype(BF16)
-    ctx_own[...] = part
-    pl.semaphore_wait(barrier, len(peers_d) + len(peers_p))
-    ctx_copies = [
-        send(ctx_send.at[p], ctx_recv.at[i], ctx_ss.at[i], ctx_rs.at[i], peers_t[i])
-        for i, p in enumerate(places)
-    ]
+    beside = jnp.where(a > 0, 1, 0) + jnp.where(a < DP - 1, 1, 0)
+    loads[0].wait()
+    ctx_copies = []
+    for n in range(K):
+        loads[1 + n].wait()
+        at = pl.ds(n * part_n, part_n)
+        part = jnp.dot(hidden[...], w_in[:, at], preferred_element_type=F32)
+        part = part.reshape(T, frames, part_n)
+        ctx_send[n] = part.astype(BF16)
+        ctx_own[n] = part
+        if n == 0:
+            pl.semaphore_wait(barrier, len(peers_p) + beside)
+        for i, p in enumerate(places):
+            ctx_copies.append(
+                send(ctx_send.at[n, p], ctx_recv.at[n, i], ctx_ss.at[n, i], ctx_rs.at[n, i],
+                     peers_t[i])
+            )
 
     rest[0].wait()
     rest[1].wait()
@@ -208,11 +210,34 @@
     rest[4].wait()
     gvec = gain[...]
 
-    ctx = ctx_own[t]
-    for i in range(T - 1):
-        got(ctx_copies[i])
-        ctx = ctx + ctx_recv[i].astype(F32)
+    for k in range(DP - 2, 0, -1):
+
+        @pl.when(a == k)
+        def _():
+            if k < DP - 2:
+                pl.semaphore_wait(above, 1)
+            pl.semaphore_signal(above, inc=1, device_id={"dp": k - 1}, device_id_type=MESH)
+            if k > 1:
+                pl.semaphore_wait(below, 1)
+            pl.semaphore_signal(below, inc=1, device_id={"dp": k + 1}, device_id_type=MESH)
+
+    halves = []
+    for n in range(K):
+        ctx = ctx_own[n, t]
+        for i in range(T - 1):
+            got(ctx_copies[n * (T - 1) + i])
+            ctx = ctx + ctx_recv[n, i].astype(F32)
+        halves.append(ctx)
+    ctx = jnp.concatenate(halves, 1)
     ctx = ctx.astype(BF16).astype(F32)
+    @pl.when(a == 0)
+    def _():
+        pl.semaphore_wait(above, 1)
+
+    @pl.when(a == DP - 1)
+    def _():
+        pl.semaphore_wait(below, 1)
+
     inputs = jnp.concatenate([ctx] * steps, 0) + jnp.concatenate(
         [jnp.zeros((frames, width), F32), gath[...]], 0
     )
@@ -257,30 +282,24 @@
         def _():
             along_dp(j, lax.rem(j - a + DP, DP) - 1, z1.at[j], rz, z1_ss, z1_rs).start()
 
-    for j0 in range(0, DP, PAIR):
-        term = lax.dot_general(
-            scaled[:, j0 * chunk : (j0 + PAIR) * chunk], gl[...], (((0,), (0,)), ((), ())),
-            preferred_element_type=F32,
-        )
-        for j in range(j0, j0 + PAIR):
-            hs[j] = term[(j - j0) * chunk : (j - j0 + 1) * chunk].astype(BF16).reshape(
-                T, S, piece, vocab
+    term = lax.dot_general(
+        scaled[...], gl[...], (((0,), (0,)), ((), ())), preferred_element_type=F32
+    )
+    hs[...] = term.astype(BF16).reshape(DP, T, S, piece, vocab)
+    for j in range(DP):
+        for e in range(1, S):
+            h1.append(
+                send(hs.at[j, :, lax.rem(s + e, S)], r1.at[j, e - 1], h1_ss.at[j, e - 1],
+                     h1_rs.at[j, e - 1], {"seq": lax.rem(s + e, S)})
             )
-            for e in range(1, S):
-                h1.append(
-                    send(hs.at[j, :, lax.rem(s + e, S)], r1.at[j, e - 1], h1_ss.at[j, e - 1],
-                         h1_rs.at[j, e - 1], {"seq": lax.rem(s + e, S)})
-                )
-
-    stat1, stat2 = [], []
-
-    def statistics():
-        total = top + jnp.log(norm)
-        nll = total - jnp.sum(logits * onehot, -1, keepdims=True)
-        left = lax.broadcasted_iota(jnp.int32, st1.shape, 1) < st1.shape[1] // 2
-        st1[...] = jnp.where(left, jnp.sum(weights * nll), jnp.sum(weights))
-        for i, peer in enumerate(peers_p):
-            stat1.append(send(st1, st1_r.at[i], st1_ss.at[i], st1_rs.at[i], peer))
+    total = top + jnp.log(norm)
+    nll = total - jnp.sum(logits * onehot, -1, keepdims=True)
+    left = lax.broadcasted_iota(jnp.int32, st1.shape, 1) < st1.shape[1] // 2
+    st1[...] = jnp.where(left, jnp.sum(weights * nll), jnp.sum(weights))
+    stat1 = [
+        send(st1, st1_r.at[i], st1_ss.at[i], st1_rs.at[i], peer) for i, peer in enumerate(peers_p)
+    ]
+    stat2 = []
 
     gc_copies = []
 
@@ -299,15 +318,6 @@
                 send(gc.at[t], gc.at[t], gc_ss.at[i], gc_rs.at[i], peers_t[i])
             )
 
-    if STAT < 0:
-        statistics()
-    for j in range(DP):
-        tensor_stage(j)
-        if j == min(STAT, DP - 1):
-            statistics()
-        if j == min(GCAT, DP - 1):
-            context_grad()
-
     z2c = []
 
     def z_stage():
@@ -322,15 +332,7 @@
         for i, p in enumerate(places):
             z2c.append(send(z2.at[p], rz2.at[i], z2_ss.at[i], z2_rs.at[i], peers_t[i]))
 
-    for j in range(DP):
-        if j == min(LAT, DP - 1):
-            stats = st1[...]
-            for i in range(len(peers_p)):
-                got(stat1[i])
-                stats = stats + st1_r[i]
-            st2[...] = stats
-            for i, peer in enumerate(peers_d):
-                stat2.append(send(st2, st2_r.at[i], st2_ss.at[i], st2_rs.at[i], peer))
+    def dp_stage(j):
         acc = s1[j, t].astype(F32)
         for i in range(T - 1):
             got(h2[j * (T - 1) + i])
@@ -345,22 +347,42 @@
             s2[j] = acc.astype(BF16)
             along_dp(j, lax.rem(j - a + DP, DP) - 1, s2.at[j], r3, h3_ss, h3_rs).start()
 
-        if j == min(ZAT, DP - 1):
-            z_stage()
-
-    for i in range(DP - 1):
-        got(stat2[i])
-        stats = stats + st2_r[i]
-    half = st1.shape[1] // 2
-    share = 1.0 / stats[0:1, half : half + 1]
-    for i in range(T - 1):
-        got(gc_copies[i])
-    product = lax.dot_general(
-        gc[...].reshape(nframes, width), w_in[...], (((1,), (1,)), ((), ())),
-        preferred_element_type=F32,
-    )
-    gh_o[...] = (product * share).astype(BF16)
-    loss_o[...] = stats * share
+    def statistics():
+        stats = st1[...]
+        for i in range(len(peers_p)):
+            got(stat1[i])
+            stats = stats + st1_r[i]
+        st2[...] = stats
+        for i, peer in enumerate(peers_d):
+            stat2.append(send(st2, st2_r.at[i], st2_ss.at[i], st2_rs.at[i], peer))
+
+    scale = []
+
+    def shares():
+        stats = st2[...]
+        for i in range(DP - 1):
+            got(stat2[i])
+            stats = stats + st2_r[i]
+        half = st1.shape[1] // 2
+        scale.append(1.0 / stats[0:1, half : half + 1])
+        loss_o[...] = stats * scale[0]
+
+    def hidden_grad():
+        for i in range(T - 1):
+            got(gc_copies[i])
+        product = lax.dot_general(
+            gc[...].reshape(nframes, width), w_in[...], (((1,), (1,)), ((), ())),
+            preferred_element_type=F32,
+        )
+        gh_o[...] = (product * scale[0]).astype(BF16)
+
+    plain = dict(J=context_grad, L=statistics, S=shares, M=hidden_grad, Z=z_stage)
+    for item in ORDER:
+        if item in plain:
+            plain[item]()
+        else:
+            dict(T=tensor_stage, K=dp_stage)[item[0]](int(item[1:]))
+    share = scale[0]
 
     groups = vocab // 128
     low = cut // 128
@@ -416,9 +438,9 @@
     scratch = [
         V(hidden.shape, BF16), V(w_in.shape, BF16), V(embed.shape, BF16), V((1, width), F32),
         V(w_head.shape, BF16), V((steps, nframes), jnp.int32), V((1, nframes), jnp.int32),
-        V((T, frames, width), F32),
-        V((T, frames, width), BF16),
-        V((T - 1, frames, width), BF16),
+        V((KCH, T, frames, width // KCH), F32),
+        V((KCH, T, frames, width // KCH), BF16),
+        V((KCH, T - 1, frames, width // KCH), BF16),
         V((rows - frames, width), F32),
         V((rows, width), BF16),
         V((rows, vocab), BF16),
@@ -437,11 +459,12 @@
         V((T, frames, width), BF16),
         V((8, 128), F32), V((T * S - 1, 8, 128), F32),
         V((8, 128), F32), V((DP - 1, 8, 128), F32),
-        dma((2 * KCH + 5,)),
-        dma((T - 1,)), dma((T - 1,)), dma((T - 1,)), dma((T - 1,)),
+        dma((KCH + 6,)),
+        dma((KCH, T - 1)), dma((KCH, T - 1)), dma((T - 1,)), dma((T - 1,)),
         dma((DP, S - 1)), dma((DP, S - 1)), dma((DP, T - 1)), dma((DP, T - 1)),
         dma((DP,)), dma((DP - 1,)), dma((DP,)), dma((DP - 1,)), dma((T - 1,)), dma((T - 1,)),
         dma((T * S - 1,)), dma((T * S - 1,)), dma((DP - 1,)), dma((DP - 1,)),
+        pltpu.SemaphoreType.REGULAR, pltpu.SemaphoreType.REGULAR,
     ]
     head_shape = jax.ShapeDtypeStruct((piece * vocab // 128, 128), F32)
     gh_shape = jax.ShapeDtypeStruct((nframes, feats), BF16)
@@ -476,11 +499,12 @@
         fits = (
             width % (16 * DP * T * S) == 0
             and width % (128 * DP) == 0
+            and width % (128 * KCH) == 0
             and vocab % 128 == 0
             and vocab > 128
             and hidden.shape[0] % (16 * T) == 0
             and min(DP, T, S) > 1
-            and DP % PAIR == 0
+            and DP == 4
         )
         run = per_device_kernel if fits else per_device_plain
         return run(hidden, w_in, embed, gain, w_head, tokens, frame_mask)

time: 21.1 us -> 20.6 us (0.976)
  Pallas kernels: 20.3 us -> 19.8 us
    pallas_call x1, Pallas kernels: 19.5 us -> 19 us  [per_device_kernel(): pl.pallas_call(functools.partial(kernel, (DP, T, S)), out_shape=(jax.Shap...]
where the time goes in v4:
time: 20.6 us; the launch traced here: 20.4 us
  Pallas kernels  19.8 us (96%)
  between operations  0.64 us (3%)
    pallas_call x1, Pallas kernels, per_device_kernel(): pl.pallas_call(functools.partial(kernel, (DP, T, S)), out_shape=(jax.Shap...  19 us
    pallas_call x1, Pallas kernels, per_device_kernel(): pl.pallas_call(write_out, out_shape=(jax.ShapeDtypeStruct((1, 1), F32), h...  0.75 us

profile of v4, /device:TPU:0, one launch (start us, length us, event | category | flops | bytes accessed | tf_op | source)
XLA Modules:
  0.0 20.4 jit_solution(18039664229799572477)
XLA Ops:
  0.6 19.0 %decode.1 = (f32[8,128]{1,0:T(8,128)S(1)}, f32[128,128]{1,0:T(8,128)S(1)}, bf16[128,1024]{1,0:T(8,128)(2,1)S(1)}) custom-call(bf16[128,1024]{1,0:T(8,128)(2,1)} %hidden_h.1, bf16[1024,512]{1,0:T(8,128)(2,1)} %w_in_h.1, bf16[1024,512]{1,0:T(8,128)(2,1)} %embed_h.1, f32[1,512]{1,0:T(1,128)} %bitcast.6, bf16[512,1024]{1,0:T(8,128)(2,1)} %w_head_h.1, ...), custom_call_target="tpu_custom_call" | custom-call | tf_op jit(solution)/shard_map/decode/pallas_call | solution.py:472
  19.7 0.7 %write_out.1 = (f32[1,1]{1,0:T(1,128)}, f32[128,128]{1,0:T(8,128)}, bf16[128,1024]{1,0:T(8,128)(2,1)}) custom-call(f32[8,128]{1,0:T(8,128)S(1)} %get-tuple-element.9.loss_i, f32[128,128]{1,0:T(8,128)S(1)} %get-tuple-element.10.head_i, bf16[128,1024]{1,0:T(8,128)(2,1)S(1)} %get-tuple-element.11.gh_i), custom_call_target="tpu_custom_call" | custom-call | tf_op jit(solution)/shard_map/write_out/pallas_call | solution.py:483
